TPU v7x, 32 devices: a whole 2x2x4 slice. The times are simulated.
32 devices in a mesh: dp: 8 (over y, x, core), fsdp: 4 (over z).
Axes of the slice: x: 2, y: 2, z: 4, core: 2. Of those that a mesh axis runs over, the one named last changes fastest.
Arguments:
- tokens: bfloat16 [16384, 1024], P(('dp', 'fsdp')), may hold values from -20 to 20
- w_qkv: bfloat16 [1024, 3072], P('fsdp'), may hold values from -0.1875 to 0.1875
- w_out: bfloat16 [1024, 1024], P('fsdp'), may hold values from -0.1875 to 0.1875
- doc_blocks: int32 [32, 4], P(('dp', 'fsdp')), may hold values from 0 to 1, never falling along the last dimension, each value on 1 to 3 neighbouring positions
- cotangent: bfloat16 [16384, 1024], P(('dp', 'fsdp')), may hold values from -6 to 6
Outputs:
- output: bfloat16 [16384, 1024], P(('dp', 'fsdp'))
- grad_tokens: bfloat16 [16384, 1024], P(('dp', 'fsdp'))
- grad_w_qkv: float32 [1024, 3072], P('fsdp')
- grad_w_out: float32 [1024, 1024], P('fsdp')
Inputs may be any that keep to these rules, and one draw needn't show every extreme that they name: `doc_blocks`: ids never fall along a sequence; each of the 2 documents of a sequence covers 1 to 3 blocks.
All inputs are finite; a program needn't handle non-finite values.
Results may differ from a plain program's by a relative error of at most 0.012.
Values may be sent and summed in bfloat16 or wider, within the bound.
A program may use at most 128 MiB of HBM per device.

v0:
```python
import functools
import math

import jax
import jax.numpy as jnp
from jax import lax
from jax.experimental import pallas as pl
from jax.experimental.pallas import tpu as pltpu
from jax.sharding import PartitionSpec as P

H = 8


NEG_FILL = -1e30
CONTRACT_ROWS = (((0,), (0,)), ((), ()))
CONTRACT_COLS = (((1,), (1,)), ((), ()))


def row_mask(doc_ids, row_count):
    block_len = row_count // doc_ids.shape[0]
    doc_rows = jnp.repeat(doc_ids, block_len, total_repeat_length=row_count)
    position = jnp.arange(row_count, dtype=jnp.int32)
    causal = position[None, :] <= position[:, None]
    return causal & (doc_rows[None, :] == doc_rows[:, None])


def split_heads(matrix, head_count):
    return matrix.reshape(matrix.shape[0], head_count, matrix.shape[1] // head_count)


def attend_forward(query_rows, key_rows, value_rows, allowed, head_count):
    row_count = query_rows.shape[0]
    query_heads = split_heads(query_rows, head_count)
    key_heads = split_heads(key_rows, head_count)
    value_heads = split_heads(value_rows, head_count)
    score_scale = query_heads.shape[2] ** (-0.5)
    scores = (
        jnp.einsum("qhd,khd->hqk", query_heads, key_heads, preferred_element_type=jnp.float32)
        * score_scale
    )
    scores = jnp.where(allowed[None], scores, NEG_FILL)
    highest = jnp.max(scores, axis=-1, keepdims=True)
    expvals = jnp.exp(scores - highest)
    attn_probs = expvals / jnp.sum(expvals, axis=-1, keepdims=True)
    probs_half = attn_probs.astype(jnp.bfloat16)
    mixed = jnp.einsum("hqk,khd->qhd", probs_half, value_heads, preferred_element_type=jnp.float32)
    return (mixed.astype(jnp.bfloat16).reshape(row_count, -1), attn_probs, probs_half)


def attend_backward(
    query_rows, key_rows, value_rows, attn_probs, probs_half, grad_mixed, head_count
):
    row_count = query_rows.shape[0]
    query_heads = split_heads(query_rows, head_count)
    key_heads = split_heads(key_rows, head_count)
    value_heads = split_heads(value_rows, head_count)
    grad_heads = split_heads(grad_mixed, head_count)
    score_scale = query_heads.shape[2] ** (-0.5)
    grad_probs = jnp.einsum(
        "qhd,khd->hqk", grad_heads, value_heads, preferred_element_type=jnp.float32
    )
    grad_values = jnp.einsum(
        "hqk,qhd->khd", probs_half, grad_heads, preferred_element_type=jnp.float32
    )
    inner = jnp.sum(attn_probs * grad_probs, axis=-1, keepdims=True)
    grad_scores = (attn_probs * (grad_probs - inner)).astype(jnp.bfloat16)
    grad_queries = (
        jnp.einsum("hqk,khd->qhd", grad_scores, key_heads, preferred_element_type=jnp.float32)
        * score_scale
    )
    grad_keys = (
        jnp.einsum("hqk,qhd->khd", grad_scores, query_heads, preferred_element_type=jnp.float32)
        * score_scale
    )
    pieces_list = [grad_queries, grad_keys, grad_values]
    return jnp.concatenate(
        [p.astype(jnp.bfloat16).reshape(row_count, -1) for p in pieces_list], axis=1
    )


def body(tokens, w_qkv, w_out, doc_blocks, cotangent):
    row_count = tokens.shape[0]
    head_width = w_out.shape[1]
    head_count = H
    all_devices = lax.axis_size("dp") * lax.axis_size("fsdp")
    allowed = row_mask(doc_blocks[0], row_count)
    columns = tokens
    qkv = jnp.dot(
        columns,
        lax.all_gather(w_qkv, "fsdp", axis=0, tiled=True),
        preferred_element_type=jnp.float32,
    ).astype(jnp.bfloat16)
    query_rows = qkv[:, :head_width]
    key_rows = qkv[:, head_width : 2 * head_width]
    value_rows = qkv[:, 2 * head_width :]
    mixed, attn_probs, probs_half = attend_forward(
        query_rows, key_rows, value_rows, allowed, head_count
    )
    output = lax.dot_general(
        mixed,
        lax.all_gather(w_out, "fsdp", axis=0, tiled=True),
        CONTRACT_COLS,
        preferred_element_type=jnp.float32,
    )
    columns = cotangent
    grad_mixed = jnp.dot(
        columns,
        lax.all_gather(w_out, "fsdp", axis=0, tiled=True),
        preferred_element_type=jnp.float32,
    ).astype(jnp.bfloat16)
    output = output.astype(jnp.bfloat16)
    grad_qkv = attend_backward(
        query_rows, key_rows, value_rows, attn_probs, probs_half, grad_mixed, head_count
    )
    grad_tokens = lax.dot_general(
        grad_qkv,
        lax.all_gather(w_qkv, "fsdp", axis=0, tiled=True),
        CONTRACT_COLS,
        preferred_element_type=jnp.float32,
    )
    grad_tokens = grad_tokens.astype(jnp.bfloat16)
    first_term = lax.dot_general(
        tokens, grad_qkv, CONTRACT_ROWS, preferred_element_type=jnp.float32
    )
    second_term = lax.dot_general(
        cotangent, mixed, CONTRACT_ROWS, preferred_element_type=jnp.float32
    )
    partial_grad = lax.psum_scatter(
        jnp.concatenate([first_term, second_term], axis=1), "fsdp", scatter_dimension=0, tiled=True
    )
    summed = lax.psum(partial_grad, "dp")
    norm_factor = 1.0 / math.sqrt(row_count * all_devices)
    grad_w_qkv = summed[:, : 3 * head_width] * norm_factor
    grad_w_out = summed[:, 3 * head_width :] * norm_factor
    return (output, grad_tokens, grad_w_qkv, grad_w_out)


MESH = pl.DeviceIdType.MESH
CHUNKS = 8


class Place:
    def __init__(self, fsdp_size):
        self.d, self.f = lax.axis_index("dp"), lax.axis_index("fsdp")
        self.c = lax.rem(self.d, 2)
        chip = lax.div(self.d, 2)
        self.x, self.y = lax.rem(chip, 2), lax.div(chip, 2)
        self.dx = self.dp_of(self.y, 1 - self.x, self.c)
        self.dy = self.dp_of(1 - self.y, self.x, self.c)
        self.dd = self.dp_of(1 - self.y, 1 - self.x, self.c)
        self.dc = self.dp_of(self.y, self.x, 1 - self.c)
        self.n = fsdp_size

    def dp_of(self, y, x, c):
        return (y * 2 + x) * 2 + c

    def ahead(self, j):
        return lax.rem(self.f + j, self.n)

    def behind(self, j):
        return lax.rem(self.f + self.n - j, self.n)

    def barrier(self):
        sem = pltpu.get_barrier_semaphore()
        targets = [(self.dx, self.f), (self.dy, self.f), (self.dc, self.f)]
        targets += [(self.d, self.ahead(j)) for j in range(1, self.n)]
        for target in targets:
            pl.semaphore_signal(sem, inc=1, device_id=target, device_id_type=MESH)
        pl.semaphore_wait(sem, len(targets))


def remote(src, dst, send_sem, recv_sem, target):
    return pltpu.make_async_remote_copy(
        src_ref=src,
        dst_ref=dst,
        send_sem=send_sem,
        recv_sem=recv_sem,
        device_id=target,
        device_id_type=MESH,
    )


def gather_kernel(n, wq_ref, wo_ref, t_ref, c_ref, fq_ref, fo_ref, tt_ref, ct_ref, send, recv, local_sem):
    me = Place(n)
    rows = wq_ref.shape[0]
    share = rows // 8
    half = share // 2
    mine, whole = (wq_ref, wo_ref), (fq_ref, fo_ref)
    me.barrier()
    started = {}

    def span(a, f, d, first, count):
        start = pl.multiple_of(f * rows + d * share + first, half)
        return whole[a].at[pl.ds(start, count)]

    def push(a, kind, j, f, d, first, count, target):
        spot = span(a, f, d, first, count)
        source = spot
        if kind == 0:
            source = mine[a].at[pl.ds(pl.multiple_of(d * share, share), share)]
        slot = kind * (n - 1) + j - 1
        copy = remote(source, spot, send.at[a, slot], recv.at[a, slot], target)
        copy.start()
        started[a, kind, j] = copy

    for j in range(1, n):
        for a in range(2):
            push(a, 0, j, me.f, me.d, 0, share, (me.d, me.ahead(j)))
    locals_ = []
    for a in range(2):
        start = pl.multiple_of(me.f * rows, rows)
        copy = pltpu.make_async_copy(mine[a], whole[a].at[pl.ds(start, rows)], local_sem.at[a])
        copy.start()
        locals_.append(copy)

    def turn(i, carry):
        part = pl.ds(pl.multiple_of(i * 128, 128), 128)
        tt_ref[part, :] = t_ref[:, part].T
        ct_ref[part, :] = c_ref[:, part].T
        return carry

    lax.fori_loop(0, t_ref.shape[1] // 128, turn, 0)
    for step in range(1, n + 2):
        for a in range(2):
            j = step
            if j < n:
                f = me.behind(j)
                started[a, 0, j].wait_recv()
                push(a, 1, j, f, me.d, 0, share, (me.dx, me.f))
                push(a, 2, j, f, me.d, 0, share, (me.dy, me.f))
                push(a, 5, j, f, me.d, 0, share, (me.dc, me.f))
            j = step - 1
            if 1 <= j < n:
                f = me.behind(j)
                started[a, 1, j].wait_recv()
                push(a, 3, j, f, me.dx, 0, half, (me.dy, me.f))
                push(a, 6, j, f, me.dx, 0, share, (me.dc, me.f))
                started[a, 2, j].wait_recv()
                push(a, 4, j, f, me.dy, half, half, (me.dx, me.f))
                push(a, 7, j, f, me.dy, 0, share, (me.dc, me.f))
            j = step - 2
            if 1 <= j < n:
                f = me.behind(j)
                started[a, 3, j].wait_recv()
                push(a, 8, j, f, me.dd, 0, half, (me.dc, me.f))
                started[a, 4, j].wait_recv()
                push(a, 9, j, f, me.dd, half, half, (me.dc, me.f))
    for (a, kind, j), copy in started.items():
        copy.wait_send()
        if kind >= 5:
            copy.wait_recv()
    for copy in locals_:
        copy.wait()


def gather_weights(n, w_qkv, w_out, tokens, cotangent):
    vmem = pl.BlockSpec(memory_space=pltpu.VMEM)
    return pl.pallas_call(
        functools.partial(gather_kernel, n),
        out_shape=[
            jax.ShapeDtypeStruct((w.shape[0] * n, w.shape[1]), w.dtype) for w in (w_qkv, w_out)
        ]
        + [jax.ShapeDtypeStruct(t.shape[::-1], t.dtype) for t in (tokens, cotangent)],
        in_specs=[vmem] * 4,
        out_specs=[pl.BlockSpec(memory_space=pl.ANY)] * 2 + [vmem] * 2,
        scratch_shapes=[
            pltpu.SemaphoreType.DMA((2, 10 * (n - 1))),
            pltpu.SemaphoreType.DMA((2, 10 * (n - 1))),
            pltpu.SemaphoreType.DMA((2,)),
        ],
        compiler_params=pltpu.CompilerParams(collective_id=0, has_side_effects=True),
        name="gather_weights",
    )(w_qkv, w_out, tokens, cotangent)


def add_half(left, right):
    return left.astype(jnp.float32) + right.astype(jnp.float32)


def reduce_kernel(
    n,
    tt_ref,
    ct_ref,
    grad_ref,
    mixed_ref,
    fq_ref,
    fo_ref,
    sum_ref,
    out_ref,
    grad_tokens_ref,
    wq,
    wo,
    grads,
    core_sum,
    pair_sum,
    plane_sum,
    z_terms,
    send,
    recv,
    local_sem,
):
    me = Place(n)
    width = 4 * mixed_ref.shape[-1] // CHUNKS
    share = grads.shape[-2]
    half = share // 2
    loads = []
    for i, (src, dst) in enumerate(((fq_ref, wq), (fo_ref, wo))):
        copy = pltpu.make_async_copy(src, dst, local_sem.at[i])
        copy.start()
        loads.append(copy)
    me.barrier()
    started = {}

    def weight_grad(k):
        def rows_of(f, carry):
            rows = pl.ds(pl.multiple_of(f * share * 8, share * 8), share * 8)
            first = k * width
            part, first = divmod(first, mixed_ref.shape[1])
            if part == 3:
                left, right = ct_ref[rows, :], mixed_ref[:, first : first + width]
            else:
                left, right = tt_ref[rows, :], grad_ref[part, :, first : first + width]
            part = jnp.dot(left, right, preferred_element_type=jnp.float32)
            grads[k, f] = part.astype(jnp.bfloat16).reshape(2, 2, 2, share, width)
            return carry

        lax.fori_loop(0, n, rows_of, 0)

    def times_weights(lefts, weight, target_ref, i):
        cols = pl.ds(i * 256, 256)
        total = None
        for p, left_ref in enumerate(lefts):
            deep = left_ref.shape[1]
            right = weight[cols, p * deep : (p + 1) * deep]
            part = lax.dot_general(
                left_ref[...], right, CONTRACT_COLS, preferred_element_type=jnp.float32
            )
            total = part if total is None else total + part
        target_ref[:, cols] = total.astype(jnp.bfloat16)

    def push(k, kind, src, dst, target):
        copy = remote(src, dst, send.at[k, kind], recv.at[k, kind], target)
        copy.start()
        started[k, kind] = copy

    def columns(k):
        return pl.ds(k * width, width)

    def core_start(k):
        push(k, 0, grads.at[k, :, :, :, 1 - me.c], core_sum.at[k], (me.dc, me.f))

    def stage_core(k):
        started[k, 0].wait_recv()

        def add(i, carry):
            f, y, x = lax.div(i, 4), lax.rem(lax.div(i, 2), 2), lax.rem(i, 2)
            total = add_half(grads[k, f, y, x, me.c], core_sum[k, f, y, x])
            core_sum[k, f, y, x] = total.astype(jnp.bfloat16)
            return carry

        lax.fori_loop(0, n * 4, add, 0)
        if k % 2 == 0:
            push(k, 1, core_sum.at[k, :, :, 1 - me.x], pair_sum.at[k], (me.dx, me.f))
        else:
            push(k, 1, core_sum.at[k, :, 1 - me.y], pair_sum.at[k], (me.dy, me.f))

    def stage_pair(k):
        started[k, 1].wait_recv()

        def add(i, carry):
            f, other = lax.div(i, 2), lax.rem(i, 2)
            own = core_sum[k, f, other, me.x] if k % 2 == 0 else core_sum[k, f, me.y, other]
            pair_sum[k, f, other] = add_half(own, pair_sum[k, f, other]).astype(jnp.bfloat16)
            return carry

        lax.fori_loop(0, n * 2, add, 0)
        if k % 2 == 0:
            push(k, 2, pair_sum.at[k, :, 1 - me.y], plane_sum.at[k], (me.dy, me.f))
        else:
            push(k, 2, pair_sum.at[k, :, 1 - me.x], plane_sum.at[k], (me.dx, me.f))

    def stage_plane(k):
        started[k, 2].wait_recv()
        keep = me.y if k % 2 == 0 else me.x

        def add(f, carry):
            plane_sum[k, f] = add_half(pair_sum[k, f, keep], plane_sum[k, f]).astype(jnp.bfloat16)
            return carry

        lax.fori_loop(0, n, add, 0)
        for j in range(1, n):
            push(k, 2 + j, plane_sum.at[k, me.ahead(j)], z_terms.at[k, j - 1], (me.d, me.ahead(j)))

    base = 2 + n

    def stage_z(k):
        total = plane_sum[k, me.f].astype(jnp.float32)
        for j in range(1, n):
            started[k, 2 + j].wait_recv()
            total = total + z_terms[k, j - 1].astype(jnp.float32)
        sum_ref[me.d, :, columns(k)] = total.astype(jnp.bfloat16)
        spot = sum_ref.at[me.d, :, columns(k)]
        push(k, base, spot, spot, (me.dx, me.f))
        push(k, base + 1, spot, spot, (me.dy, me.f))
        push(k, base + 4, spot, spot, (me.dc, me.f))

    def stage_spread(k):
        started[k, base].wait_recv()
        spot = sum_ref.at[me.dx, pl.ds(0, half), columns(k)]
        push(k, base + 2, spot, spot, (me.dy, me.f))
        spot = sum_ref.at[me.dx, :, columns(k)]
        push(k, base + 5, spot, spot, (me.dc, me.f))
        started[k, base + 1].wait_recv()
        spot = sum_ref.at[me.dy, pl.ds(half, half), columns(k)]
        push(k, base + 3, spot, spot, (me.dx, me.f))
        spot = sum_ref.at[me.dy, :, columns(k)]
        push(k, base + 6, spot, spot, (me.dc, me.f))

    def stage_last(k):
        started[k, base + 2].wait_recv()
        spot = sum_ref.at[me.dd, pl.ds(0, half), columns(k)]
        push(k, base + 7, spot, spot, (me.dc, me.f))
        started[k, base + 3].wait_recv()
        spot = sum_ref.at[me.dd, pl.ds(half, half), columns(k)]
        push(k, base + 8, spot, spot, (me.dc, me.f))

    order = [CHUNKS - 1, CHUNKS - 2] + list(range(CHUNKS - 2))
    stages = (
        (0, weight_grad),
        (1, core_start),
        (2, stage_core),
        (4, stage_pair),
        (6, stage_plane),
        (8, stage_z),
        (9, stage_spread),
        (10, stage_last),
    )
    lefts = [grad_ref.at[p] for p in range(3)]
    pieces = [(lefts, wq, grad_tokens_ref, i) for i in range(wq.shape[0] // 256)]
    pieces += [([mixed_ref], wo, out_ref, i) for i in range(wo.shape[0] // 256)]
    for step in range(CHUNKS + 10):
        for after, stage in stages:
            if 0 <= step - after < CHUNKS:
                stage(order[step - after])
        if step == 2:
            for copy in loads:
                copy.wait()
        if step >= 2 and pieces:
            times_weights(*pieces.pop(0))
    for piece in pieces:
        times_weights(*piece)
    for (k, kind), copy in started.items():
        copy.wait_send()
        if kind >= base + 4:
            copy.wait_recv()


def reduce_grads(n, tokens_t, cotangent_t, grad_qkv, mixed, full_qkv, full_out):
    features, rows = tokens_t.shape
    share = features // (n * 8)
    width = 4 * mixed.shape[1] // CHUNKS
    kinds = 2 + n + 9
    vmem = pl.BlockSpec(memory_space=pltpu.VMEM)
    anywhere = pl.BlockSpec(memory_space=pl.ANY)
    return pl.pallas_call(
        functools.partial(reduce_kernel, n),
        out_shape=[
            jax.ShapeDtypeStruct((8, share, CHUNKS * width), jnp.bfloat16),
            jax.ShapeDtypeStruct((rows, features), jnp.bfloat16),
            jax.ShapeDtypeStruct((rows, features), jnp.bfloat16),
        ],
        in_specs=[vmem] * 4 + [anywhere] * 2,
        out_specs=[vmem] * 3,
        scratch_shapes=[
            pltpu.VMEM(full_qkv.shape, jnp.bfloat16),
            pltpu.VMEM(full_out.shape, jnp.bfloat16),
            pltpu.VMEM((CHUNKS, n, 2, 2, 2, share, width), jnp.bfloat16),
            pltpu.VMEM((CHUNKS, n, 2, 2, share, width), jnp.bfloat16),
            pltpu.VMEM((CHUNKS, n, 2, share, width), jnp.bfloat16),
            pltpu.VMEM((CHUNKS, n, share, width), jnp.bfloat16),
            pltpu.VMEM((CHUNKS, n - 1, share, width), jnp.bfloat16),
            pltpu.SemaphoreType.DMA((CHUNKS, kinds)),
            pltpu.SemaphoreType.DMA((CHUNKS, kinds)),
            pltpu.SemaphoreType.DMA((2,)),
        ],
        compiler_params=pltpu.CompilerParams(
            collective_id=1, has_side_effects=True, vmem_limit_bytes=54 << 20
        ),
        name="reduce_grads",
    )(tokens_t, cotangent_t, grad_qkv, mixed, full_qkv, full_out)


def attend_kernel(mask_ref, q_ref, k_ref, v_ref, gm_ref, mixed_ref, grad_ref):
    q, k, v, gm = q_ref[...], k_ref[...], v_ref[...], gm_ref[...]
    scale = q.shape[1] ** (-0.5)

    def dot(left, right, dims):
        return lax.dot_general(left, right, dims, preferred_element_type=jnp.float32)

    plain = (((1,), (0,)), ((), ()))
    scores = jnp.where(mask_ref[...] > 0.0, dot(q, k, CONTRACT_COLS) * scale, NEG_FILL)
    expvals = jnp.exp(scores - jnp.max(scores, axis=-1, keepdims=True))
    probs = expvals / jnp.sum(expvals, axis=-1, keepdims=True)
    probs_half = probs.astype(jnp.bfloat16)
    mixed_ref[...] = dot(probs_half, v, plain).astype(jnp.bfloat16)
    grad_probs = dot(gm, v, CONTRACT_COLS)
    inner = jnp.sum(probs * grad_probs, axis=-1, keepdims=True)
    grad_scores = (probs * (grad_probs - inner)).astype(jnp.bfloat16)
    grad_ref[0] = (dot(grad_scores, k, plain) * scale).astype(jnp.bfloat16)
    grad_ref[1] = (dot(grad_scores, q, CONTRACT_ROWS) * scale).astype(jnp.bfloat16)
    grad_ref[2] = dot(probs_half, gm, CONTRACT_ROWS).astype(jnp.bfloat16)


def attend(mask, qkv, grad_mixed, head_count):
    rows, width = grad_mixed.shape
    size = width // head_count

    def column(first):
        return pl.BlockSpec((rows, size), lambda h: (0, first + h))

    return pl.pallas_call(
        attend_kernel,
        grid=(head_count,),
        out_shape=[
            jax.ShapeDtypeStruct((rows, width), jnp.bfloat16),
            jax.ShapeDtypeStruct((3, rows, width), jnp.bfloat16),
        ],
        in_specs=[
            pl.BlockSpec((rows, rows), lambda h: (0, 0)),
            column(0),
            column(head_count),
            column(2 * head_count),
            column(0),
        ],
        out_specs=[column(0), pl.BlockSpec((3, rows, size), lambda h: (0, 0, h))],
        compiler_params=pltpu.CompilerParams(vmem_limit_bytes=48 << 20),
        name="attend",
    )(mask, qkv, qkv, qkv, grad_mixed)


def chip_body(tokens, w_qkv, w_out, doc_blocks, cotangent):
    row_count = tokens.shape[0]
    head_width = w_out.shape[1]
    n = lax.axis_size("fsdp")
    all_devices = lax.axis_size("dp") * n
    allowed = row_mask(doc_blocks[0], row_count)
    full_qkv, full_out, tokens_t, cotangent_t = gather_weights(
        n, w_qkv, w_out, tokens, cotangent
    )
    qkv = jnp.dot(tokens, full_qkv, preferred_element_type=jnp.float32).astype(jnp.bfloat16)
    grad_mixed = jnp.dot(cotangent, full_out, preferred_element_type=jnp.float32)
    grad_mixed = grad_mixed.astype(jnp.bfloat16)
    mixed, grad_qkv = attend(allowed.astype(jnp.float32), qkv, grad_mixed, H)
    summed, output, grad_tokens = reduce_grads(
        n, tokens_t, cotangent_t, grad_qkv, mixed, full_qkv, full_out
    )
    summed = summed.reshape(w_out.shape[0], 4 * head_width).astype(jnp.float32)
    norm_factor = 1.0 / math.sqrt(row_count * all_devices)
    grad_w_qkv = summed[:, : 3 * head_width] * norm_factor
    grad_w_out = summed[:, 3 * head_width :] * norm_factor
    return (output, grad_tokens, grad_w_qkv, grad_w_out)


def solution(mesh):
    placed = (
        P(("dp", "fsdp"), None),
        P("fsdp", None),
        P("fsdp", None),
        P(("dp", "fsdp"), None),
        P(("dp", "fsdp"), None),
    )
    in_plane = mesh.shape["dp"] == 8 and mesh.shape["fsdp"] == 4
    return jax.shard_map(
        chip_body if in_plane else body,
        mesh=mesh,
        in_specs=placed,
        out_specs=(
            P(("dp", "fsdp"), None),
            P(("dp", "fsdp"), None),
            P("fsdp", None),
            P("fsdp", None),
        ),
        check_vma=False,
    )
```

profile of v0, /device:TPU:0, one launch (start us, length us, event | category | flops | bytes accessed | tf_op | source)
XLA Modules:
  0.0 162.8 jit_solution(6402798261494071252)
XLA Ops:
  0.6 0.0 copy-start.4
  0.7 1.4 fusion.6
  2.1 2.6 %compare_select_fusion.1 = s32[512,1]{0,1:T(1,128)S(1)} fusion(s32[512,1]{0,1:T(1,128)S(1)} %bitcast.27, s32[512,1]{0,1:T(1,128)S(1)} %bitcast.26, s32[]{:T(128)} %bitcast.4, s32[]{:T(128)} %bitcast.5, s32[]{:T(128)} %bitcast.7, s32[]{:T(128)} %bitcast.6), kind=kLoop, calls=%fused_computation.11 | loop fusion | flops 4096 | bytes 6160 | tf_op jit(solution)/shard_map/jit(_take)/gather | solution.py:21
  4.7 0.2 fusion.3.mask_ref
  4.9 0.0 copy-start.5
  4.9 51.3 %gather_weights.1 = (bf16[1024,3072]{1,0:T(8,128)(2,1)}, bf16[1024,1024]{1,0:T(8,128)(2,1)}, bf16[1024,512]{1,0:T(8,128)(2,1)}, bf16[1024,512]{1,0:T(8,128)(2,1)}) custom-call(bf16[256,3072]{1,0:T(8,128)(2,1)} %wq_ref.1, bf16[256,1024]{1,0:T(8,128)(2,1)} %wo_ref.1, bf16[512,1024]{1,0:T(8,128)(2,1)} %t_ref.1, bf16[512,1024]{1,0:T(8,128)(2,1)} %c_ref.1), custom_call_target="tpu_custom_call" | custom-call | tf_op jit(solution)/shard_map/gather_weights/pallas_call | solution.py:258
  56.1 0.0 copy-done.4
  56.1 0.0 copy-start.1
  56.2 3.0 %fusion.1.gm_ref = bf16[512,1024]{1,0:T(8,128)(2,1)S(1)} fusion(bf16[512,1024]{1,0:T(8,128)(2,1)S(1)} %copy-done.4, bf16[1024,1024]{1,0:T(8,128)(2,1)} %get-tuple-element.28.fo_ref), kind=kOutput, calls=%fused_computation.5 | convolution fusion | flops 1074266112 | bytes 4194304 | tf_op jit(solution)/shard_map/dot_general | solution.py:551
  59.2 0.0 copy-done.5
  59.2 0.4 copy-done.1
  59.6 4.8 %fusion.q_ref.k_ref.v_ref = bf16[512,3072]{1,0:T(8,128)(2,1)} fusion(bf16[512,1024]{1,0:T(8,128)(2,1)S(1)} %copy-done.5, bf16[1024,3072]{1,0:T(8,128)(2,1)S(1)} %copy-done.1), kind=kOutput, calls=%fused_computation.1 | convolution fusion | flops 3222798336 | bytes 10485760 | tf_op jit(solution)/shard_map/dot_general | solution.py:550
  64.3 15.3 %attend.1 = (bf16[512,1024]{1,0:T(8,128)(2,1)S(1)}, bf16[3,512,1024]{2,1,0:T(8,128)(2,1)}) custom-call(f32[512,512]{1,0:T(8,128)S(1)} %fusion.3.mask_ref, bf16[512,3072]{1,0:T(8,128)(2,1)} %fusion.q_ref.k_ref.v_ref, bf16[512,3072]{1,0:T(8,128)(2,1)} %fusion.q_ref.k_ref.v_ref, bf16[512,3072]{1,0:T(8,128)(2,1)} %fusion.q_ref.k_ref.v_ref, ...), custom_call_target="tpu_custom_call" | custom-call | tf_op jit(solution)/shard_map/attend/pallas_call | solution.py:521
  79.6 0.0 copy-start
  79.6 1.0 copy-done
  80.6 75.2 %reduce_grads.1 = (bf16[8,32,4096]{2,1,0:T(8,128)(2,1)}, bf16[512,1024]{1,0:T(8,128)(2,1)}, bf16[512,1024]{1,0:T(8,128)(2,1)}) custom-call(bf16[1024,512]{1,0:T(8,128)(2,1)} %get-tuple-element.25.tt_ref, bf16[1024,512]{1,0:T(8,128)(2,1)} %get-tuple-element.26.ct_ref, bf16[3,512,1024]{2,1,0:T(8,128)(2,1)} %get-tuple-element.29.grad_ref, ...), custom_call_target="tpu_custom_call" | custom-call | tf_op jit(solution)/shard_map/reduce_grads/pallas_call | solution.py:465
  155.8 2.1 %bitcast_convert_fusion = f32[256,4096]{1,0:T(8,128)S(1)} fusion(bf16[8,32,4096]{2,1,0:T(8,128)(2,1)} %get-tuple-element.33), kind=kLoop, calls=%fused_computation.3 | loop fusion | flops 1048576 | bytes 6291456 | tf_op jit(solution)/shard_map/convert_element_type | solution.py:557
  157.9 1.1 slice_multiply_fusion.1
  158.9 0.0 copy-start.3
  158.9 0.0 copy-start.2
  158.9 1.9 %slice_multiply_fusion = f32[256,3072]{1,0:T(8,128)} fusion(f32[256,4096]{1,0:T(8,128)S(1)} %bitcast_convert_fusion), kind=kLoop, calls=%fused_computation.2 | loop fusion | flops 786432 | bytes 6291456 | tf_op jit(solution)/shard_map/mul | solution.py:559
  160.8 0.0 copy-done.3
  160.8 1.0 copy.15
  161.8 0.0 copy-done.2
  161.8 1.0 copy.16
  (3 shorter events, 0.0 us)
Async XLA Ops:
  0.6 55.5 %copy-start.4 = (bf16[512,1024]{1,0:T(8,128)(2,1)S(1)}, bf16[512,1024]{1,0:T(8,128)(2,1)}, u32[]{:S(2)}) copy-start(bf16[512,1024]{1,0:T(8,128)(2,1)} %c_ref.1) | copy-start | bytes 3145732
  4.9 54.3 %copy-start.5 = (bf16[512,1024]{1,0:T(8,128)(2,1)S(1)}, bf16[512,1024]{1,0:T(8,128)(2,1)}, u32[]{:S(2)}) copy-start(bf16[512,1024]{1,0:T(8,128)(2,1)} %t_ref.1) | copy-start | bytes 3145732
  56.1 3.4 %copy-start.1 = (bf16[1024,3072]{1,0:T(8,128)(2,1)S(1)}, bf16[1024,3072]{1,0:T(8,128)(2,1)}, u32[]{:S(2)}) copy-start(bf16[1024,3072]{1,0:T(8,128)(2,1)} %get-tuple-element.27.fq_ref) | copy-start | bytes 18874372
  79.6 1.0 copy-start
  158.9 1.9 %copy-start.3 = (bf16[512,1024]{1,0:T(8,128)(2,1)S(1)}, bf16[512,1024]{1,0:T(8,128)(2,1)}, u32[]{:S(2)}) copy-start(bf16[512,1024]{1,0:T(8,128)(2,1)} %get-tuple-element.42) | copy-start | bytes 3145732
  158.9 2.9 %copy-start.2 = (bf16[512,1024]{1,0:T(8,128)(2,1)S(1)}, bf16[512,1024]{1,0:T(8,128)(2,1)}, u32[]{:S(2)}) copy-start(bf16[512,1024]{1,0:T(8,128)(2,1)} %get-tuple-element.43) | copy-start | bytes 3145732
where the time goes:
time: 163 us
  Pallas kernels  142 us (87%)
  other arithmetic  7.81 us (5%)
  matrix products  7.76 us (5%)
  local copies, waits for them, and re-layouts  4.72 us (3%)
    pallas_call x1, Pallas kernels, reduce_grads(): pl.pallas_call(functools.partial(reduce_kernel, n), out_shape=[jax.ShapeD...  75.2 us
    pallas_call x1, Pallas kernels, gather_weights(): pl.pallas_call(functools.partial(gather_kernel, n), out_shape=[jax.ShapeD...  51.3 us
    pallas_call x1, Pallas kernels, attend(): pl.pallas_call(attend_kernel, grid=(head_count,), out_shape=[jax.ShapeDty...  15.3 us
    dot_general x1, matrix products, chip_body(): jnp.dot(tokens, full_qkv, preferred_element_type=jnp.float32)  4.77 us
    unnamed x14, local copies, waits for them, and re-layouts  3.33 us

commit v1 on v0

v1 whole, which is shorter than its diff:
```python
import functools
import math

import jax
import jax.numpy as jnp
from jax import lax
from jax.experimental import pallas as pl
from jax.experimental.pallas import tpu as pltpu
from jax.sharding import PartitionSpec as P

H = 8


NEG_FILL = -1e30
CONTRACT_ROWS = (((0,), (0,)), ((), ()))
CONTRACT_COLS = (((1,), (1,)), ((), ()))


def row_mask(doc_ids, row_count):
    block_len = row_count // doc_ids.shape[0]
    doc_rows = jnp.repeat(doc_ids, block_len, total_repeat_length=row_count)
    position = jnp.arange(row_count, dtype=jnp.int32)
    causal = position[None, :] <= position[:, None]
    return causal & (doc_rows[None, :] == doc_rows[:, None])


def split_heads(matrix, head_count):
    return matrix.reshape(matrix.shape[0], head_count, matrix.shape[1] // head_count)


def attend_forward(query_rows, key_rows, value_rows, allowed, head_count):
    row_count = query_rows.shape[0]
    query_heads = split_heads(query_rows, head_count)
    key_heads = split_heads(key_rows, head_count)
    value_heads = split_heads(value_rows, head_count)
    score_scale = query_heads.shape[2] ** (-0.5)
    scores = (
        jnp.einsum("qhd,khd->hqk", query_heads, key_heads, preferred_element_type=jnp.float32)
        * score_scale
    )
    scores = jnp.where(allowed[None], scores, NEG_FILL)
    highest = jnp.max(scores, axis=-1, keepdims=True)
    expvals = jnp.exp(scores - highest)
    attn_probs = expvals / jnp.sum(expvals, axis=-1, keepdims=True)
    probs_half = attn_probs.astype(jnp.bfloat16)
    mixed = jnp.einsum("hqk,khd->qhd", probs_half, value_heads, preferred_element_type=jnp.float32)
    return (mixed.astype(jnp.bfloat16).reshape(row_count, -1), attn_probs, probs_half)


def attend_backward(
    query_rows, key_rows, value_rows, attn_probs, probs_half, grad_mixed, head_count
):
    row_count = query_rows.shape[0]
    query_heads = split_heads(query_rows, head_count)
    key_heads = split_heads(key_rows, head_count)
    value_heads = split_heads(value_rows, head_count)
    grad_heads = split_heads(grad_mixed, head_count)
    score_scale = query_heads.shape[2] ** (-0.5)
    grad_probs = jnp.einsum(
        "qhd,khd->hqk", grad_heads, value_heads, preferred_element_type=jnp.float32
    )
    grad_values = jnp.einsum(
        "hqk,qhd->khd", probs_half, grad_heads, preferred_element_type=jnp.float32
    )
    inner = jnp.sum(attn_probs * grad_probs, axis=-1, keepdims=True)
    grad_scores = (attn_probs * (grad_probs - inner)).astype(jnp.bfloat16)
    grad_queries = (
        jnp.einsum("hqk,khd->qhd", grad_scores, key_heads, preferred_element_type=jnp.float32)
        * score_scale
    )
    grad_keys = (
        jnp.einsum("hqk,qhd->khd", grad_scores, query_heads, preferred_element_type=jnp.float32)
        * score_scale
    )
    pieces_list = [grad_queries, grad_keys, grad_values]
    return jnp.concatenate(
        [p.astype(jnp.bfloat16).reshape(row_count, -1) for p in pieces_list], axis=1
    )


def body(tokens, w_qkv, w_out, doc_blocks, cotangent):
    row_count = tokens.shape[0]
    head_width = w_out.shape[1]
    head_count = H
    all_devices = lax.axis_size("dp") * lax.axis_size("fsdp")
    allowed = row_mask(doc_blocks[0], row_count)
    columns = tokens
    qkv = jnp.dot(
        columns,
        lax.all_gather(w_qkv, "fsdp", axis=0, tiled=True),
        preferred_element_type=jnp.float32,
    ).astype(jnp.bfloat16)
    query_rows = qkv[:, :head_width]
    key_rows = qkv[:, head_width : 2 * head_width]
    value_rows = qkv[:, 2 * head_width :]
    mixed, attn_probs, probs_half = attend_forward(
        query_rows, key_rows, value_rows, allowed, head_count
    )
    output = lax.dot_general(
        mixed,
        lax.all_gather(w_out, "fsdp", axis=0, tiled=True),
        CONTRACT_COLS,
        preferred_element_type=jnp.float32,
    )
    columns = cotangent
    grad_mixed = jnp.dot(
        columns,
        lax.all_gather(w_out, "fsdp", axis=0, tiled=True),
        preferred_element_type=jnp.float32,
    ).astype(jnp.bfloat16)
    output = output.astype(jnp.bfloat16)
    grad_qkv = attend_backward(
        query_rows, key_rows, value_rows, attn_probs, probs_half, grad_mixed, head_count
    )
    grad_tokens = lax.dot_general(
        grad_qkv,
        lax.all_gather(w_qkv, "fsdp", axis=0, tiled=True),
        CONTRACT_COLS,
        preferred_element_type=jnp.float32,
    )
    grad_tokens = grad_tokens.astype(jnp.bfloat16)
    first_term = lax.dot_general(
        tokens, grad_qkv, CONTRACT_ROWS, preferred_element_type=jnp.float32
    )
    second_term = lax.dot_general(
        cotangent, mixed, CONTRACT_ROWS, preferred_element_type=jnp.float32
    )
    partial_grad = lax.psum_scatter(
        jnp.concatenate([first_term, second_term], axis=1), "fsdp", scatter_dimension=0, tiled=True
    )
    summed = lax.psum(partial_grad, "dp")
    norm_factor = 1.0 / math.sqrt(row_count * all_devices)
    grad_w_qkv = summed[:, : 3 * head_width] * norm_factor
    grad_w_out = summed[:, 3 * head_width :] * norm_factor
    return (output, grad_tokens, grad_w_qkv, grad_w_out)


MESH = pl.DeviceIdType.MESH


class Place:
    def __init__(self, fsdp_size):
        self.d, self.f = lax.axis_index("dp"), lax.axis_index("fsdp")
        self.c = lax.rem(self.d, 2)
        chip = lax.div(self.d, 2)
        self.x, self.y = lax.rem(chip, 2), lax.div(chip, 2)
        self.dx = self.dp_of(self.y, 1 - self.x, self.c)
        self.dy = self.dp_of(1 - self.y, self.x, self.c)
        self.dd = self.dp_of(1 - self.y, 1 - self.x, self.c)
        self.dc = self.dp_of(self.y, self.x, 1 - self.c)
        self.n = fsdp_size

    def dp_of(self, y, x, c):
        return (y * 2 + x) * 2 + c

    def ahead(self, j):
        return lax.rem(self.f + j, self.n)

    def behind(self, j):
        return lax.rem(self.f + self.n - j, self.n)

    def barrier(self):
        sem = pltpu.get_barrier_semaphore()
        targets = [(self.dx, self.f), (self.dy, self.f), (self.dc, self.f)]
        targets += [(self.d, self.ahead(j)) for j in range(1, self.n)]
        for target in targets:
            pl.semaphore_signal(sem, inc=1, device_id=target, device_id_type=MESH)
        pl.semaphore_wait(sem, len(targets))


def remote(src, dst, send_sem, recv_sem, target):
    return pltpu.make_async_remote_copy(
        src_ref=src,
        dst_ref=dst,
        send_sem=send_sem,
        recv_sem=recv_sem,
        device_id=target,
        device_id_type=MESH,
    )


(
    GZ, GX, GY, GC, GXY, GYX, GCX, GCY, GCD, GCE,
    RC, PX, PY, QX, QY, RZ,
    SX, SY, SC, SXY, SYX, SCX, SCY, SCD, SCE,
) = (0, 3, 4, 5, 6, 7, 8, 9, 10, 11, 12, 13, 14, 15, 16, 17, 20, 21, 22, 23, 24, 25, 26, 27, 28)
KINDS = 29
LEAD = 3
PLAIN = (((1,), (0,)), ((), ()))


def add_half(left, right):
    return (left.astype(jnp.float32) + right.astype(jnp.float32)).astype(jnp.bfloat16)


def dot(left, right, dims=PLAIN):
    return lax.dot_general(left, right, dims, preferred_element_type=jnp.float32)


def layer_kernel(
    n,
    doc_ref,
    tok_any,
    cot_any,
    wq_any,
    wo_any,
    sumq_any,
    sumo_any,
    out_any,
    gt_any,
    tok,
    cot,
    tok_t,
    cot_t,
    w,
    bias,
    x,
    g,
    grads,
    core_sum,
    pair_x,
    pair_y,
    plane,
    z_terms,
    sums,
    result,
    send,
    recv,
    w_sem,
    in_sem,
    sum_sem,
    res_sem,
):
    me = Place(n)
    rows, feat = tok.shape
    share = w.shape[3]
    mid = share // 2
    size = w.shape[4] // 4
    wide = 3 * size
    block = feat // n
    low, high = pl.ds(0, mid), pl.ds(mid, mid)
    others = pl.ds(1, n - 1)

    def spot_of(r):
        return pl.ds(pl.multiple_of(me.ahead(r) * block, block), block)

    def w_load(h, p):
        if p == 3:
            src = wo_any.at[:, :, pl.ds(pl.multiple_of(h * size, size), size)]
        else:
            first = pl.multiple_of(p * H * size + h * size, size)
            src = wq_any.at[:, :, pl.ds(first, size)]
        dst = w.at[h, 0, :, :, pl.ds(p * size, size)]
        return pltpu.make_async_copy(src, dst, w_sem.at[h, p])

    def in_load(i, r):
        src, dst = ((tok_any, tok), (cot_any, cot))[i]
        return pltpu.make_async_copy(
            src.at[:, spot_of(r)], dst.at[:, pl.ds(r * block, block)], in_sem.at[i, r]
        )

    def sum_store(h, p):
        if p == 3:
            dst = sumo_any.at[:, :, pl.ds(pl.multiple_of(h * size, size), size)]
        else:
            first = pl.multiple_of(p * H * size + h * size, size)
            dst = sumq_any.at[:, :, pl.ds(first, size)]
        return pltpu.make_async_copy(
            sums.at[h, :, :, pl.ds(p * size, size)], dst, sum_sem.at[h, p]
        )

    def res_store(i, r):
        dst = (gt_any, out_any)[i].at[:, spot_of(r)]
        return pltpu.make_async_copy(result.at[i, r], dst, res_sem.at[i, r])

    def make(h, kind, src, dst, target):
        return remote(src, dst, send.at[h, kind], recv.at[h, kind], target)

    to_x, to_y, to_c = (me.dx, me.f), (me.dy, me.f), (me.dc, me.f)

    def copy(h, kind, j=0):
        if kind == GZ:
            return make(
                h, GZ + j - 1, w.at[h, 0, me.d], w.at[h, n - j, me.d], (me.d, me.ahead(j))
            )
        if kind == RZ:
            return make(h, RZ + j - 1, plane.at[h, j], z_terms.at[h, j - 1], (me.d, me.ahead(j)))
        if kind == RC:
            return make(h, kind, grads.at[h, :, :, :, 1 - me.c], core_sum.at[h], to_c)
        if kind == PX:
            src = core_sum.at[h, :, :, 1 - me.x, low]
            return make(h, kind, src, pair_x.at[h], to_x)
        if kind == PY:
            src = core_sum.at[h, :, 1 - me.y, :, high]
            return make(h, kind, src, pair_y.at[h], to_y)
        if kind == QX:
            return make(h, kind, pair_x.at[h, :, 1 - me.y], plane.at[h, :, low], to_y)
        if kind == QY:
            return make(h, kind, pair_y.at[h, :, 1 - me.x], plane.at[h, :, high], to_x)
        if kind < RC:
            def at(d, part=None):
                return w.at[h, others, d] if part is None else w.at[h, others, d, part]
        else:
            def at(d, part=None):
                return sums.at[h, d] if part is None else sums.at[h, d, part]
        spot, target = {
            GX: (at(me.d), to_x),
            GY: (at(me.d), to_y),
            GC: (at(me.d), to_c),
            GXY: (at(me.dx, low), to_y),
            GYX: (at(me.dy, high), to_x),
            GCX: (at(me.dx), to_c),
            GCY: (at(me.dy), to_c),
            GCD: (at(me.dd, low), to_c),
            GCE: (at(me.dd, high), to_c),
        }[kind if kind < RC else kind - SX + GX]
        return make(h, kind, spot, spot, target)

    def spread(h, base):
        for kind in (GX, GY, GC):
            copy(h, base + kind).start()

    def forward(h, base):
        copy(h, base + GX).wait_recv()
        copy(h, base + GXY).start()
        copy(h, base + GCX).start()
        copy(h, base + GY).wait_recv()
        copy(h, base + GYX).start()
        copy(h, base + GCY).start()

    def across(h, base):
        copy(h, base + GXY).wait_recv()
        copy(h, base + GCD).start()
        copy(h, base + GYX).wait_recv()
        copy(h, base + GCE).start()

    def collect(h, base):
        for kind in (GC, GCX, GCY, GCD, GCE):
            copy(h, base + kind).wait_recv()

    def gather_spread(h):
        for j in range(1, n):
            copy(h, GZ, j).wait_recv()
        spread(h, 0)

    def gather_forward(h):
        forward(h, 0)

    def gather_across(h):
        across(h, 0)

    def project(h):
        collect(h, 0)
        x[:, :wide] = dot(
            tok[...], w[h, :, :, :, :wide].reshape(feat, wide)
        ).astype(jnp.bfloat16)
        x[:, wide:] = dot(
            cot[...], w[h, :, :, :, wide:].reshape(feat, size)
        ).astype(jnp.bfloat16)

    def attend(h):
        scale = size ** (-0.5)
        half = rows // 2
        parts = []
        for first, keys in ((0, half), (half, rows)):
            mine = slice(first, first + half)
            q, k = x[mine, :size], x[:keys, size : 2 * size]
            v, gm = x[:keys, 2 * size : wide], x[mine, wide:]
            scores = dot(q, k, CONTRACT_COLS) * scale + bias[mine, :keys]
            expvals = jnp.exp(scores - jnp.max(scores, axis=-1, keepdims=True))
            probs = expvals * (1.0 / jnp.sum(expvals, axis=-1, keepdims=True))
            probs_half = probs.astype(jnp.bfloat16)
            g[h, mine, wide:] = dot(probs_half, v).astype(jnp.bfloat16)
            grad_probs = dot(gm, v, CONTRACT_COLS)
            inner = jnp.sum(probs * grad_probs, axis=-1, keepdims=True)
            grad_scores = (probs * (grad_probs - inner)).astype(jnp.bfloat16)
            g[h, mine, :size] = (dot(grad_scores, k) * scale).astype(jnp.bfloat16)
            parts.append((dot(grad_scores, q, CONTRACT_ROWS), dot(probs_half, gm, CONTRACT_ROWS)))
        for i, factor in ((0, scale), (1, 1.0)):
            cols = slice((i + 1) * size, (i + 2) * size)
            early, late = parts[0][i], parts[1][i]
            g[h, :half, cols] = ((early + late[:half]) * factor).astype(jnp.bfloat16)
            g[h, half:, cols] = (late[half:] * factor).astype(jnp.bfloat16)

    def weight_grad(h):
        def some(r, carry):
            part = pl.ds(pl.multiple_of(r * block, block), block)
            shape = (2, 2, 2, share)
            left = dot(tok_t[part, :], g[h, :, :wide]).astype(jnp.bfloat16)
            grads[h, r, :, :, :, :, :wide] = left.reshape(*shape, wide)
            right = dot(cot_t[part, :], g[h, :, wide:]).astype(jnp.bfloat16)
            grads[h, r, :, :, :, :, wide:] = right.reshape(*shape, size)
            return carry

        lax.fori_loop(0, n, some, 0)
        copy(h, RC).start()

    def core_add(h):
        copy(h, RC).wait_recv()

        def some(r, carry):
            core_sum[h, r] = add_half(grads[h, r, :, :, me.c], core_sum[h, r])
            return carry

        lax.fori_loop(0, n, some, 0)
        copy(h, PX).start()
        copy(h, PY).start()

    def pair_add(h):
        copy(h, PX).wait_recv()
        pair_x[h] = add_half(core_sum[h, :, :, me.x, :mid], pair_x[h])
        copy(h, QX).start()
        copy(h, PY).wait_recv()
        pair_y[h] = add_half(core_sum[h, :, me.y, :, mid:], pair_y[h])
        copy(h, QY).start()

    def plane_add(h):
        copy(h, QX).wait_recv()
        plane[h, :, :mid] = add_half(pair_x[h, :, me.y], plane[h, :, :mid])
        copy(h, QY).wait_recv()
        plane[h, :, mid:] = add_half(pair_y[h, :, me.x], plane[h, :, mid:])
        for j in range(1, n):
            copy(h, RZ, j).start()

    def line_add(h):
        total = plane[h, 0].astype(jnp.float32)
        for j in range(1, n):
            copy(h, RZ, j).wait_recv()
            total = total + z_terms[h, j - 1].astype(jnp.float32)
        sums[h, me.d] = total.astype(jnp.bfloat16)
        spread(h, SX - GX)

    def sum_forward(h):
        forward(h, SX - GX)

    def sum_across(h):
        across(h, SX - GX)

    def sum_finish(h):
        collect(h, SX - GX)
        for p in range(4):
            sum_store(h, p).start()

    def token_piece(r):
        total = None
        for h in range(H):
            right = w[h, r, :, :, :wide].reshape(block, wide)
            part = dot(g[h, :, :wide], right, CONTRACT_COLS)
            total = part if total is None else total + part
        result[0, r] = total.astype(jnp.bfloat16)
        res_store(0, r).start()

    def output_piece(r):
        total = None
        for h in range(H):
            right = w[h, r, :, :, wide:].reshape(block, size)
            part = dot(g[h, :, wide:], right, CONTRACT_COLS)
            total = part if total is None else total + part
        result[1, r] = total.astype(jnp.bfloat16)
        res_store(1, r).start()

    for h in range(H):
        for p in range(4):
            w_load(h, p).start()
    for i in range(2):
        for r in range(n):
            in_load(i, r).start()
    me.barrier()
    for h in range(H):
        for p in range(4):
            w_load(h, p).wait()
        for j in range(1, n):
            copy(h, GZ, j).start()
    docs = [doc_ref[0, b] for b in range(doc_ref.shape[1])]
    length = rows // len(docs)

    def doc_of(index):
        found = jnp.full(index.shape, docs[0], jnp.int32)
        for b in range(1, len(docs)):
            found = jnp.where(index >= b * length, docs[b], found)
        return found

    def fill(i, carry):
        first = pl.multiple_of(i * 128, 128)
        row = lax.broadcasted_iota(jnp.int32, (128, 1), 0) + first
        col = lax.broadcasted_iota(jnp.int32, (1, rows), 1)
        allowed = (col <= row) & (doc_of(row) == doc_of(col))
        bias[pl.ds(first, 128), :] = jnp.where(allowed, 0.0, NEG_FILL)
        return carry

    lax.fori_loop(0, rows // 128, fill, 0)
    for i in range(2):
        for r in range(n):
            in_load(i, r).wait()

    def turn(i, carry):
        part = pl.ds(pl.multiple_of(i * 128, 128), 128)
        tok_t[part, :] = tok[:, part].T
        cot_t[part, :] = cot[:, part].T
        return carry

    lax.fori_loop(0, feat // 128, turn, 0)

    stages = (
        (0, H, gather_spread),
        (1, H, gather_forward),
        (2, H, gather_across),
        (LEAD + 1, H, core_add),
        (LEAD, H, project),
        (LEAD + 2, H, pair_add),
        (LEAD + 4, H, plane_add),
        (LEAD, H, attend),
        (LEAD + 5, H, line_add),
        (LEAD + 6, H, sum_forward),
        (LEAD, H, weight_grad),
        (LEAD + 7, H, sum_across),
        (LEAD + H, n, token_piece),
        (LEAD + H, n, output_piece),
        (LEAD + 8, H, sum_finish),
    )

    def step(t, carry):
        for after, count, stage in stages:
            k = t - after
            pl.when((k >= 0) & (k < count))(functools.partial(stage, k))
        return carry

    lax.fori_loop(0, LEAD + 8 + H, step, 0)

    def finish(h, carry):
        for kind in range(KINDS):
            if GZ <= kind < GX:
                copy(h, GZ, kind - GZ + 1).wait_send()
            elif RZ <= kind < SX:
                copy(h, RZ, kind - RZ + 1).wait_send()
            else:
                copy(h, kind).wait_send()
        for p in range(4):
            sum_store(h, p).wait()
        return carry

    lax.fori_loop(0, H, finish, 0)
    for i in range(2):
        for r in range(n):
            res_store(i, r).wait()


def layer(n, tokens, cotangent, w_qkv, w_out, doc_blocks):
    rows, feat = tokens.shape
    shard, head_width = w_out.shape
    share, size = shard // 8, head_width // H
    wide = 4 * size
    half = jnp.bfloat16
    anywhere = pl.BlockSpec(memory_space=pl.ANY)
    w_qkv = w_qkv.reshape(8, share, 3 * head_width)
    w_out = w_out.reshape(8, share, head_width)
    sumq, sumo, output, grad_tokens = pl.pallas_call(
        functools.partial(layer_kernel, n),
        out_shape=[
            jax.ShapeDtypeStruct(w_qkv.shape, half),
            jax.ShapeDtypeStruct(w_out.shape, half),
            jax.ShapeDtypeStruct((rows, feat), half),
            jax.ShapeDtypeStruct((rows, feat), half),
        ],
        in_specs=[pl.BlockSpec(memory_space=pltpu.SMEM)] + [anywhere] * 4,
        out_specs=[anywhere] * 4,
        scratch_shapes=[
            pltpu.VMEM((rows, feat), half),
            pltpu.VMEM((rows, feat), half),
            pltpu.VMEM((feat, rows), half),
            pltpu.VMEM((feat, rows), half),
            pltpu.VMEM((H, n, 8, share, wide), half),
            pltpu.VMEM((rows, rows), jnp.float32),
            pltpu.VMEM((rows, wide), half),
            pltpu.VMEM((H, rows, wide), half),
            pltpu.VMEM((H, n, 2, 2, 2, share, wide), half),
            pltpu.VMEM((H, n, 2, 2, share, wide), half),
            pltpu.VMEM((H, n, 2, share // 2, wide), half),
            pltpu.VMEM((H, n, 2, share // 2, wide), half),
            pltpu.VMEM((H, n, share, wide), half),
            pltpu.VMEM((H, n - 1, share, wide), half),
            pltpu.VMEM((H, 8, share, wide), half),
            pltpu.VMEM((2, n, rows, feat // n), half),
            pltpu.SemaphoreType.DMA((H, KINDS)),
            pltpu.SemaphoreType.DMA((H, KINDS)),
            pltpu.SemaphoreType.DMA((H, 4)),
            pltpu.SemaphoreType.DMA((2, n)),
            pltpu.SemaphoreType.DMA((H, 4)),
            pltpu.SemaphoreType.DMA((2, n)),
        ],
        compiler_params=pltpu.CompilerParams(
            collective_id=0, has_side_effects=True, vmem_limit_bytes=60 << 20
        ),
        name="layer",
    )(doc_blocks, tokens, cotangent, w_qkv, w_out)
    return sumq.reshape(shard, 3 * head_width), sumo.reshape(shard, head_width), output, grad_tokens


def chip_body(tokens, w_qkv, w_out, doc_blocks, cotangent):
    n = lax.axis_size("fsdp")
    all_devices = lax.axis_size("dp") * n
    sumq, sumo, output, grad_tokens = layer(n, tokens, cotangent, w_qkv, w_out, doc_blocks)
    norm_factor = 1.0 / math.sqrt(tokens.shape[0] * all_devices)
    grad_w_qkv = sumq.astype(jnp.float32) * norm_factor
    grad_w_out = sumo.astype(jnp.float32) * norm_factor
    return (output, grad_tokens, grad_w_qkv, grad_w_out)


def solution(mesh):
    placed = (
        P(("dp", "fsdp"), None),
        P("fsdp", None),
        P("fsdp", None),
        P(("dp", "fsdp"), None),
        P(("dp", "fsdp"), None),
    )
    in_plane = mesh.shape["dp"] == 8 and mesh.shape["fsdp"] == 4
    return jax.shard_map(
        chip_body if in_plane else body,
        mesh=mesh,
        in_specs=placed,
        out_specs=(
            P(("dp", "fsdp"), None),
            P(("dp", "fsdp"), None),
            P("fsdp", None),
            P("fsdp", None),
        ),
        check_vma=False,
    )
```

time: 163 us -> 111 us (0.68)
  Pallas kernels: 142 us -> 103 us
  matrix products: 7.76 us -> 0 us
  other arithmetic: 7.81 us -> 4.67 us
  local copies, waits for them, and re-layouts: 4.72 us -> 1.95 us
    pallas_call x3 -> x1, Pallas kernels: 142 us -> 103 us  [layer(): pl.pallas_call(functools.partial(layer_kernel, n), out_shape=[jax.ShapeDt...]
    dot_general x2 -> x0, matrix products: 7.76 us -> none  [the longest x1 4.77 us: chip_body(): jnp.dot(tokens, full_qkv, preferred_element_type=jnp.float32)]
    gather x1 -> x0, other arithmetic: 2.59 us -> none  [row_mask(): doc_rows = jnp.repeat(doc_ids, block_len, total_repeat_length=row_count)]
    convert_element_type x2 -> x0, other arithmetic: 2.24 us -> none  [the longest x1 2.06 us: chip_body(): summed = summed.reshape(w_out.shape[0], 4 * head_width).astype(jnp.float32)]
    mul x2, other arithmetic: 2.95 us -> 4.67 us  [the longest x1 3.58 us: chip_body(): grad_w_qkv = sumq.astype(jnp.float32) * norm_factor]
    unnamed x14 -> x8, local copies, waits for them, and re-layouts: 3.33 us -> 1.95 us
where the time goes in v1:
time: 111 us
  Pallas kernels  103 us (93%)
  other arithmetic  4.67 us (4%)
  local copies, waits for them, and re-layouts  1.95 us (2%)
    pallas_call x1, Pallas kernels, layer(): pl.pallas_call(functools.partial(layer_kernel, n), out_shape=[jax.ShapeDt...  103 us
    mul x1, other arithmetic, chip_body(): grad_w_qkv = sumq.astype(jnp.float32) * norm_factor  3.58 us

profile of v1, /device:TPU:0, one launch (start us, length us, event | category | flops | bytes accessed | tf_op | source)
XLA Modules:
  0.0 110.6 jit_solution(1113740708834988132)
XLA Ops:
  0.6 103.3 %layer.1 = (bf16[8,32,3072]{2,1,0:T(8,128)(2,1)}, bf16[8,32,1024]{2,1,0:T(8,128)(2,1)}, bf16[512,1024]{1,0:T(8,128)(2,1)}, bf16[512,1024]{1,0:T(8,128)(2,1)}) custom-call(s32[1,4]{1,0:T(1,128)} %doc_ref.1, bf16[512,1024]{1,0:T(8,128)(2,1)} %tok_any.1, bf16[512,1024]{1,0:T(8,128)(2,1)} %cot_any.1, bf16[8,32,3072]{2,1,0:T(8,128)(2,1)} %bitcast.5, ...), custom_call_target="tpu_custom_call" | custom-call | tf_op jit(solution)/shard_map/layer/pallas_call | solution.py:557
  103.9 0.0 copy-start.2
  104.0 0.0 copy-start.1
  104.0 0.0 copy-start
  104.0 3.6 %convert_multiply_fusion = f32[8,32,3072]{2,1,0:T(8,128)} fusion(bf16[8,32,3072]{2,1,0:T(8,128)(2,1)} %get-tuple-element.10), kind=kLoop, calls=%fused_computation | loop fusion | flops 1572864 | bytes 4718592 | tf_op jit(solution)/shard_map/mul | solution.py:604
  107.6 0.0 copy-done.2
  107.6 1.1 convert_multiply_fusion.1
  108.6 0.0 copy-done.1
  108.7 1.0 copy.11
  109.6 0.0 copy-done
  109.6 1.0 copy.12
Async XLA Ops:
  103.9 3.6 %copy-start.2 = (bf16[8,32,1024]{2,1,0:T(8,128)(2,1)S(1)}, bf16[8,32,1024]{2,1,0:T(8,128)(2,1)}, u32[]{:S(2)}) copy-start(bf16[8,32,1024]{2,1,0:T(8,128)(2,1)} %get-tuple-element.11) | copy-start | bytes 1572868
  104.0 4.7 %copy-start.1 = (bf16[512,1024]{1,0:T(8,128)(2,1)S(1)}, bf16[512,1024]{1,0:T(8,128)(2,1)}, u32[]{:S(2)}) copy-start(bf16[512,1024]{1,0:T(8,128)(2,1)} %get-tuple-element.16) | copy-start | bytes 3145732
  104.0 5.7 %copy-start = (bf16[512,1024]{1,0:T(8,128)(2,1)S(1)}, bf16[512,1024]{1,0:T(8,128)(2,1)}, u32[]{:S(2)}) copy-start(bf16[512,1024]{1,0:T(8,128)(2,1)} %get-tuple-element.17) | copy-start | bytes 3145732
